TPU v7x, 256 devices: a whole 4x4x8 slice. The times are simulated.
256 devices in a mesh: seq: 64 (over z, x, y_lo), head: 4 (over y_hi, core).
Axes of the slice: x: 4, y: 4 (y_hi: 2, y_lo: 2; y = y_hi * 2 + y_lo), z: 8, core: 2. Of those that a mesh axis runs over, the one named last changes fastest.
Arguments:
- query: bfloat16 [8192, 3072], P('seq', 'head'), may hold values from -256 to 256
- keys: bfloat16 [8192, 3072], P('seq', 'head'), may hold values from -4 to 4
- values: bfloat16 [8192, 3072], P('seq', 'head'), may hold values from -5 to 5
- out_weight: bfloat16 [3072, 4096], P('head'), may hold values from -0.109375 to 0.109375
- image_start: int32 [3], replicated, may hold values from 0 to 7168, as said below
Outputs:
- mixed: bfloat16 [8192, 4096], P('seq', 'head')
Inputs may be any that keep to these rules, and one draw needn't show every extreme that they name: `image_start`: the starts increase; each image's 1024 positions lie inside the sequence and no two images share a position; the last image ends at the sequence's end.
All inputs are finite; a program needn't handle non-finite values.
Results may differ from a plain program's by a relative error of at most 0.012.
Values may be sent and summed in bfloat16 or wider, within the bound.
A program may use at most 192 MiB of HBM per device.

v0:
```python
import jax
import jax.numpy as jnp
from jax import lax
from jax.sharding import PartitionSpec as P

HEAD_DIM = 128


def image_tags(positions, image_start, patch_count):
    inside = (positions[:, None] >= image_start[None, :]) & (
        positions[:, None] < image_start[None, :] + patch_count
    )
    labels = jnp.arange(image_start.shape[0], dtype=jnp.int32) + 1
    return jnp.sum(jnp.where(inside, labels[None, :], 0), axis=1) - 1


def body(query, keys, values, out_weight, image_start):
    cycle_size = lax.axis_size("seq")
    own_index = lax.axis_index("seq")
    row_count = query.shape[0]
    seq_total = row_count * cycle_size
    patch_count = min(1024, seq_total // 8)
    head_count = query.shape[1] // HEAD_DIM
    scale = HEAD_DIM ** (-0.5)
    query_pos = own_index * row_count + jnp.arange(row_count, dtype=jnp.int32)
    query_heads = jnp.transpose(query.reshape(row_count, head_count, HEAD_DIM), (1, 0, 2))
    query_tag = image_tags(query_pos, image_start, patch_count)
    initial = (
        jnp.full((head_count, row_count), -1e30, jnp.float32),
        jnp.zeros((head_count, row_count), jnp.float32),
        jnp.zeros((head_count, row_count, HEAD_DIM), jnp.float32),
    )
    key_major = jnp.transpose(keys.reshape(row_count, head_count, HEAD_DIM), (1, 0, 2))
    value_major = jnp.transpose(values.reshape(row_count, head_count, HEAD_DIM), (1, 0, 2))
    key_value = jnp.stack((key_major, value_major))
    block_pair = lax.all_gather(key_value, "seq", axis=2, tiled=True)
    piece_len = block_pair.shape[2]
    key_pos = jnp.arange(piece_len, dtype=jnp.int32)
    key_tag = image_tags(key_pos, image_start, patch_count)
    in_range = (key_pos >= 0) & (key_pos < seq_total)
    visible = in_range[None, :] & (
        (key_pos[None, :] <= query_pos[:, None])
        | (query_tag[:, None] == key_tag[None, :]) & (query_tag[:, None] >= 0)
    )

    def compute(state_old):
        row_high, row_sum, weighted = state_old
        key_block = block_pair[0]
        value_block = block_pair[1]
        scores = (
            jnp.einsum("hqd,hkd->hqk", query_heads, key_block, preferred_element_type=jnp.float32)
            * scale
        )
        scores = jnp.where(visible[None], scores, -1e30)
        new_high = jnp.maximum(row_high, jnp.max(scores, axis=-1))
        weights = jnp.where(visible[None], jnp.exp(scores - new_high[..., None]), 0.0)
        row_sum = jnp.sum(weights, axis=-1)
        update = jnp.einsum(
            "hqk,hkd->hqd",
            weights.astype(jnp.bfloat16),
            value_block,
            preferred_element_type=jnp.float32,
        )
        weighted = update
        return (new_high, row_sum, weighted)

    def unchanged(state_old):
        return state_old

    state_now = lax.cond(jnp.any(visible), compute, unchanged, initial)
    row_high, row_sum, weighted = state_now
    attended = (weighted / row_sum[..., None]).astype(jnp.bfloat16)
    attended_rows = jnp.transpose(attended, (1, 0, 2)).reshape(row_count, head_count * HEAD_DIM)
    partial_value = jnp.dot(attended_rows, out_weight, preferred_element_type=jnp.float32)
    return lax.psum_scatter(
        partial_value.astype(jnp.bfloat16), "head", scatter_dimension=1, tiled=True
    )


def solution(mesh):
    placed = (P("seq", "head"), P("seq", "head"), P("seq", "head"), P("head", None), P())
    return jax.shard_map(
        body, mesh=mesh, in_specs=placed, out_specs=P("seq", "head"), check_vma=False
    )
```

profile of v0, /device:TPU:1, one launch (start us, length us, event | category | flops | bytes accessed | tf_op | source)
XLA Modules:
  0.0 784.2 jit_solution(2414290603275093940)
XLA Ops:
  6.5 0.0 all-gather.2.cloned.1.call-start
  6.5 1.1 copy.12
  7.6 1.1 copy.13
  8.7 0.8 pad_maximum_fusion
  9.6 0.0 all-gather.2.cloned.1.call-update
  9.6 0.0 reduce-scatter.2.cloned.1.call-start
  9.6 1.1 copy.14
  10.8 0.7 iota_add_fusion
  11.4 0.7 select_reduce_fusion.1
  12.2 0.8 select_reduce_fusion
  13.0 2.6 fusion.16
  16.3 603.2 %all-gather.2.cloned.1.call-done = bf16[2,6,8192,128]{2,3,1,0:T(8,128)(2,1)} async-done(((bf16[2,6,128,128]{2,3,1,0:T(8,128)(2,1)}), bf16[2,6,8192,128]{2,3,1,0:T(8,128)(2,1)}) %all-gather.2.cloned.1.call-update) | async-done | bytes 25165840 | tf_op jit(solution)/shard_map/all_gather | solution.py:36
  619.5 74.4 %conditional.1 = (f32[6,128]{1,0:T(8,128)S(1)}, f32[6,128,128]{1,2,0:T(8,128)S(1)}) conditional(s32[]{:T(128)} %convert_element_type.12, () %tuple.13, (pred[128,8192]{1,0:T(8,128)(4,1)S(1)}, bf16[2,6,8192,128]{2,3,1,0:T(8,128)(2,1)}, bf16[6,128,128]{1,2,0:T(8,128)(2,1)S(1)}) %tuple.28), branch_computations={%region_3.4_spmd, %region_4.7_spmd} | conditional | flops 3303013632 | bytes 154748944 | solution.py:70
  619.5 32.6 %copy.15 = bf16[2,6,8192,128]{3,2,1,0:T(8,128)(2,1)} copy(bf16[2,6,8192,128]{2,3,1,0:T(8,128)(2,1)} %get-tuple-element.22) | data formatting | bytes 50331648 | tf_op jit(solution)/shard_map
  652.1 13.6 %fusion = (f32[6,128]{1,0:T(8,128)S(1)}, f32[6,128,8192]{2,1,0:T(8,128)}) fusion(pred[128,8192]{1,0:T(8,128)(4,1)S(1)} %get-tuple-element.11, bf16[6,128,128]{1,2,0:T(8,128)(2,1)S(1)} %get-tuple-element.23, bf16[2,6,8192,128]{3,2,1,0:T(8,128)(2,1)} %copy.15), kind=kOutput, calls=%fused_computation.2 | convolution fusion | flops 1629486336 | bytes 38996992 | tf_op jit(solution)/shard_map/cond/branch_1_fun/hqd,hkd->hqk/dot_general | solution.py:51
  665.7 15.8 %fusion.3 = f32[6,128,128]{1,2,0:T(8,128)S(1)} fusion(bf16[2,6,8192,128]{3,2,1,0:T(8,128)(2,1)} %copy.15, f32[6,128,8192]{2,1,0:T(8,128)} %get-tuple-element.28, f32[6,128]{1,0:T(8,128)S(1)} %broadcast_maximum_fusion, pred[128,8192]{1,0:T(8,128)(4,1)S(1)} %get-tuple-element.11), kind=kOutput, calls=%fused_computation.6 | convolution fusion | flops 1642070016 | bytes 39193600 | tf_op jit(solution)/shard_map/cond | solution.py:70
  681.4 12.5 %fusion.2 = f32[6,128]{1,0:T(8,128)S(1)} fusion(f32[6,128,8192]{2,1,0:T(8,128)} %get-tuple-element.28, f32[6,128]{1,0:T(8,128)S(1)} %broadcast_maximum_fusion, pred[128,8192]{1,0:T(8,128)(4,1)S(1)} %get-tuple-element.11), kind=kLoop, calls=%fused_computation.4 | loop fusion | flops 31456512 | bytes 26220544 | tf_op jit(solution)/shard_map/cond/branch_1_fun/reduce_sum | solution.py:57
  693.9 4.8 convolution_convert_fusion
  698.7 0.0 reduce-scatter.2.cloned.1.call-update
  698.8 78.6 %reduce-scatter.2.cloned.1.call-done = bf16[128,1024]{1,0:T(8,128)(2,1)} async-done(((bf16[128,4096]{1,0:T(8,128)(2,1)}), bf16[128,1024]{1,0:T(8,128)(2,1)}) %reduce-scatter.2.cloned.1.call-update) | async-done | bytes 262160 | tf_op jit(solution)/shard_map/reduce_scatter | solution.py:75
  (7 shorter events, 0.1 us)
Async XLA Ops:
  6.5 612.9 %all-gather.2.cloned.1.call-start = ((), (), s32[]{:S(2)}) async-start(), calls=%async_computation.1 | async-start | bytes 25559040 | tf_op jit(solution)/shard_map/all_gather | solution.py:36
  9.6 767.8 %reduce-scatter.2.cloned.1.call-start = ((), (), s32[]{:S(2)}) async-start(), calls=%async_computation.2 | async-start | bytes 1310720 | tf_op jit(solution)/shard_map/reduce_scatter | solution.py:75
Sparse Core Ops, SparseCore 0:
  9.7 609.7 all-gather.1
  698.9 78.4 reduce-scatter.1
where the time goes:
time: 785 us; the launch traced here: 784 us
  waiting for transfers between devices  682 us (87%)
  local copies, waits for them, and re-layouts  35.8 us (5%)
  matrix products  34.2 us (4%)
  other arithmetic  18.2 us (2%)
  between operations  14.1 us (2%)
    all_gather x1, waiting for transfers between devices, body(): block_pair = lax.all_gather(key_value, 'seq', axis=2, tiled=True)  603 us
    reduce_scatter x1, waiting for transfers between devices, body(): lax.psum_scatter(partial_value.astype(jnp.bfloat16), 'head', scatter_dime...  78.6 us
    another operation x1, local copies, waits for them, and re-layouts  32.6 us
    cond x1, matrix products, body(): state_now = lax.cond(jnp.any(visible), compute, unchanged, initial)  15.8 us
  transfers between devices with their start and end apart: 2, of which 2 were waited for; matrix products, arithmetic and copies ran while one was open for 1% of the time, Pallas kernels for 0%

commit v1 on v0

v1 whole, which is shorter than its diff:
```python
import math

import jax
import jax.numpy as jnp
from jax import lax
from jax.experimental import pallas as pl
from jax.experimental.pallas import tpu as pltpu
from jax.sharding import PartitionSpec as P

MESH = pl.DeviceIdType.MESH
HD = 128
PATCHES = 1024
NEG = -1e30
SCALE = HD**-0.5 * math.log2(math.e)


def place():
    s, h = lax.axis_index("seq"), lax.axis_index("head")
    return s // 8, (s // 2) % 4, s % 2, h // 2, h % 2


def device(z, x, yl, yh, c):
    return ((z * 4 + x) * 2 + yl, yh * 2 + c)


def kernel(
    start_ref, q_ref, k_ref, v_ref, w_ref, o_ref,
    vt, kv, qb, accs, ms, ls, lims, ot, att_t, att, wv, own, pair_out, pair_in, cross_out, cross_in,
    a_send, a_kv, a_q, x_send, x_recv, f_send, f_recv, p_send, p_recv, o_send, o_recv, w_sem, r_send, r_recv,
):
    z, x, yl, yh, c = place()
    active = z % 4 != 3
    home_core = z // 4
    head = 2 * (z % 4) + yl
    right, left = (x + 1) % 4, (x + 3) % 4
    opposite = (x + 2) % 4
    to_right = device(z, right, yl, yh, c)
    to_left = device(z, left, yl, yh, c)
    to_pair = device(z, x, yl, yh, 1 - c)
    to_cross = device(z, x, yl, 1 - yh, c)

    def worker(i):
        return 4 * c + i // 2, i % 2

    def is_own(i):
        wz, wyl = worker(i)
        return (wz == z) & (wyl == yl) & (yl == c)

    def source_is_own(zs):
        return (zs == z) & (yl == c) & (home_core == c)

    barrier = pltpu.get_barrier_semaphore()

    def greet(dev):
        pl.semaphore_signal(barrier, inc=1, device_id=dev, device_id_type=MESH)

    def greet_worker(i, _):
        wz, wyl = worker(i)

        @pl.when(jnp.logical_not(is_own(i)))
        def _():
            greet(device(wz, x, wyl, yh, yl))

        return 0

    lax.fori_loop(0, 6, greet_worker, 0)
    greet(to_pair)
    greet(to_cross)

    @pl.when(active)
    def _():
        greet(to_right)
        greet(to_left)

        def greet_source(zs, _):
            @pl.when(jnp.logical_not(source_is_own(zs)))
            def _():
                greet(device(zs, x, c, yh, home_core))

            return 0

        lax.fori_loop(0, 8, greet_source, 0)

    w_copy = pltpu.make_async_copy(w_ref, wv, w_sem)
    w_copy.start()
    for i in range(6):
        vt[i] = v_ref[:, i * HD : (i + 1) * HD].T
    for zq in range(8):
        pos = ((zq * 4 + x) * 2 + c) * HD + lax.broadcasted_iota(jnp.int32, (1, HD), 1)
        lim = pos
        for n in range(3):
            first = start_ref[n]
            lim = jnp.where((pos >= first) & (pos < first + PATCHES), first + (PATCHES - 1), lim)
        lims[zq] = jnp.broadcast_to(lim, (8, HD))

    own_pair = ((yl == c) & (home_core == c) & active).astype(jnp.int32)
    expected = 8 + jnp.where(active, 10, 0) - 2 * own_pair
    pl.semaphore_wait(barrier, expected)

    slot = (z * 4 + x) * 2 + yl

    def pieces(i):
        columns = pl.ds(i * HD, HD)
        return (
            (k_ref.at[:, columns], kv.at[0, slot], a_kv.at[z]),
            (vt.at[i], kv.at[1, slot], a_kv.at[z]),
            (q_ref.at[:, columns], qb.at[z], a_q.at[z]),
        )

    def a_copy(i, n):
        wz, wyl = worker(i)
        src, dst, sem = pieces(i)[n]
        return pltpu.make_async_remote_copy(
            src, dst, a_send.at[n, i], sem, device_id=device(wz, x, wyl, yh, yl), device_id_type=MESH
        )

    def a_local(i, n):
        src, dst, sem = pieces(i)[n]
        return pltpu.make_async_copy(src, dst, sem)

    def a_start(i, ns):
        @pl.when(is_own(i))
        def _():
            for n in ns:
                a_local(i, n).start()

        @pl.when(jnp.logical_not(is_own(i)))
        def _():
            for n in ns:
                a_copy(i, n).start()

    for i in range(6):
        a_start(i, (0, 1))
    for i in range(6):
        a_start(i, (2,))

    @pl.when(active)
    def _():
        def at(zk, xk, w):
            return (zk * 4 + xk) * 2 + w

        def nearest(d):
            off = jnp.where(d % 2 == 1, (d + 1) // 2, 8 - d // 2)
            return (z + off) % 8

        def x_copy(side, b):
            s = at(b, x, c)
            return pltpu.make_async_remote_copy(
                kv.at[:, s], kv.at[:, s], x_send.at[side, b], x_recv.at[side, b],
                device_id=to_right if side == 0 else to_left, device_id_type=MESH,
            )

        def x_wait(side, b):
            s = at(b, left if side == 0 else right, c)
            pltpu.make_async_remote_copy(
                kv.at[:, s], kv.at[:, s], x_send.at[side, b], x_recv.at[side, b],
                device_id=to_right if side == 0 else to_left, device_id_type=MESH,
            ).wait_recv()

        def f_copy(side, b):
            s = at(b, left if side == 0 else right, c)
            return pltpu.make_async_remote_copy(
                kv.at[side, s], kv.at[side, s], f_send.at[side, b], f_recv.at[side, b],
                device_id=to_right if side == 0 else to_left, device_id_type=MESH,
            )

        def f_wait(side, b):
            s = at(b, opposite, c)
            pltpu.make_async_remote_copy(
                kv.at[side, s], kv.at[side, s], f_send.at[side, b], f_recv.at[side, b],
                device_id=to_right if side == 0 else to_left, device_id_type=MESH,
            ).wait_recv()

        def p_copy(rel, b, w):
            s = at(b, (x + rel) % 4, w)
            return pltpu.make_async_remote_copy(
                kv.at[:, s], kv.at[:, s], p_send.at[rel, b], p_recv.at[rel, b], device_id=to_pair, device_id_type=MESH
            )

        def own_step(d, _):
            b = nearest(d)
            s = at(b, x, c)
            pltpu.make_async_remote_copy(
                kv.at[:, s], kv.at[:, s], x_send.at[0, b], a_kv.at[b], device_id=to_pair, device_id_type=MESH
            ).wait_recv()
            x_copy(0, b).start()
            x_copy(1, b).start()
            p_copy(0, b, c).start()
            return 0

        def side_step(d, _):
            b = nearest(d)
            x_wait(0, b)
            f_copy(0, b).start()
            p_copy(3, b, c).start()
            x_wait(1, b)
            f_copy(1, b).start()
            p_copy(1, b, c).start()
            return 0

        def far_step(d, _):
            b = nearest(d)
            f_wait(0, b)
            f_wait(1, b)
            p_copy(2, b, c).start()
            return 0

        def pair_wait(rel):
            def step(b, _):
                p_copy(rel, b, 1 - c).wait_recv()
                return 0

            lax.fori_loop(0, 8, step, 0)

        def q_wait(b, _):
            pltpu.make_async_remote_copy(
                qb.at[b], qb.at[b], x_send.at[0, b], a_q.at[b], device_id=to_pair, device_id_type=MESH
            ).wait_recv()
            return 0

        rows = lax.broadcasted_iota(jnp.int32, (4 * HD, HD), 0)
        rows = jnp.where(rows >= 2 * HD, rows + (8 * HD - 2 * HD), rows)

        def attend(xk, zq, carry, masked):
            def step(n, carry):
                m, l, acc = carry
                s0 = at(2 * n, xk, 0)
                k = jnp.concatenate([kv[0, s0], kv[0, s0 + 1], kv[0, s0 + 8], kv[0, s0 + 9]], axis=0)
                v = jnp.concatenate([kv[1, s0], kv[1, s0 + 1], kv[1, s0 + 8], kv[1, s0 + 9]], axis=1)
                sc = lax.dot_general(k, qb[zq], (((1,), (1,)), ((), ())), preferred_element_type=jnp.float32) * SCALE
                if masked:
                    sc = jnp.where(rows <= lims[zq, 0:1] - s0 * HD, sc, NEG)
                m_new = jnp.maximum(m, jnp.max(sc, axis=0, keepdims=True))
                p = jnp.exp2(sc - m_new)
                alpha = jnp.exp2(m - m_new)
                l = l * alpha + jnp.sum(p, axis=0, keepdims=True)
                acc = acc * alpha + jnp.dot(v, p.astype(jnp.bfloat16), preferred_element_type=jnp.float32)
                return m_new, l, acc

            first = zq // 2
            if masked:
                return lax.fori_loop(first, jnp.minimum((zq + 1) // 2, 3) + 1, step, carry)
            return lax.fori_loop(0, first, step, carry)

        def stage(rels, last):
            def per_q(zq, _):
                carry = (ms[zq, 0:1], ls[zq, 0:1], accs[zq])
                for rel in rels:
                    xk = (x + rel) % 4
                    carry = attend(xk, zq, carry, False)
                    carry = attend(xk, zq, carry, True)
                m, l, acc = carry
                if last:
                    ot[zq] = (acc * (1.0 / l)).astype(jnp.bfloat16)
                    own_source = source_is_own(zq)

                    @pl.when(own_source)
                    def _():
                        pltpu.make_async_copy(ot.at[zq], att_t.at[head], o_recv.at[head]).start()

                    @pl.when(jnp.logical_not(own_source))
                    def _():
                        o_copy(zq).start()
                else:
                    ms[zq] = jnp.broadcast_to(m, (8, HD))
                    ls[zq] = jnp.broadcast_to(l, (8, HD))
                    accs[zq] = acc
                return 0

            lax.fori_loop(0, 8, per_q, 0)

        def o_copy(zq):
            return pltpu.make_async_remote_copy(
                ot.at[zq], att_t.at[head], o_send.at[zq], o_recv.at[head],
                device_id=device(zq, x, c, yh, home_core), device_id_type=MESH,
            )

        ms[...] = jnp.full_like(ms, NEG)
        ls[...] = jnp.zeros_like(ls)
        accs[...] = jnp.zeros_like(accs)
        lax.fori_loop(0, 8, own_step, 0)
        lax.fori_loop(0, 8, q_wait, 0)
        lax.fori_loop(0, 8, side_step, 0)
        pair_wait(0)
        stage((0,), False)
        lax.fori_loop(0, 8, far_step, 0)
        pair_wait(3)
        pair_wait(1)
        stage((3, 1), False)
        pair_wait(2)
        stage((2,), True)

        def drain(b, _):
            for side in (0, 1):
                x_copy(side, b).wait_send()
                f_copy(side, b).wait_send()
            for rel in range(4):
                p_copy(rel, b, c).wait_send()

            @pl.when(jnp.logical_not(source_is_own(b)))
            def _():
                o_copy(b).wait_send()

            return 0

        lax.fori_loop(0, 8, drain, 0)

    for i in range(6):
        pltpu.make_async_remote_copy(
            att_t.at[i], att_t.at[i], a_send.at[0, i], o_recv.at[i], device_id=to_pair, device_id_type=MESH
        ).wait_recv()
        att[:, i * HD : (i + 1) * HD] = att_t[i].T

    w_copy.wait()
    width = o_ref.shape[1]

    def project(gy, gc):
        first = pl.multiple_of((gy * 2 + gc) * width, width)
        return jnp.dot(att[...], wv[:, pl.ds(first, width)], preferred_element_type=jnp.float32)

    def pair_copy(n):
        return pltpu.make_async_remote_copy(
            pair_out.at[n], pair_in.at[n], r_send.at[n], r_recv.at[n], device_id=to_pair, device_id_type=MESH
        )

    cross = pltpu.make_async_remote_copy(
        cross_out, cross_in, r_send.at[2], r_recv.at[2], device_id=to_cross, device_id_type=MESH
    )
    pair_out[0] = project(1 - yh, 1 - c).astype(jnp.bfloat16)
    pair_copy(0).start()
    own[...] = project(1 - yh, c)
    pair_copy(0).wait_recv()
    cross_out[...] = (own[...] + pair_in[0].astype(jnp.float32)).astype(jnp.bfloat16)
    cross.start()
    pair_out[1] = project(yh, 1 - c).astype(jnp.bfloat16)
    pair_copy(1).start()
    own[...] = project(yh, c)
    pair_copy(1).wait_recv()
    own[...] += pair_in[1].astype(jnp.float32)
    cross.wait_recv()
    o_ref[...] = (own[...] + cross_in[...].astype(jnp.float32)).astype(jnp.bfloat16)
    pair_copy(0).wait_send()
    pair_copy(1).wait_send()
    cross.wait_send()
    for i in range(6):

        @pl.when(jnp.logical_not(is_own(i)))
        def _():
            for n in range(3):
                a_copy(i, n).wait_send()


def body(query, keys, values, out_weight, image_start):
    rows, depth = query.shape
    width = out_weight.shape[1] // lax.axis_size("head")
    bf, f32, dma = jnp.bfloat16, jnp.float32, pltpu.SemaphoreType.DMA
    vmem = pl.BlockSpec(memory_space=pltpu.VMEM)
    return pl.pallas_call(
        kernel,
        out_shape=jax.ShapeDtypeStruct((rows, width), bf),
        in_specs=[pl.BlockSpec(memory_space=pltpu.SMEM), vmem, vmem, vmem, pl.BlockSpec(memory_space=pl.ANY)],
        out_specs=vmem,
        scratch_shapes=[
            pltpu.VMEM((6, HD, HD), bf),
            pltpu.VMEM((2, 64, HD, HD), bf),
            pltpu.VMEM((8, HD, HD), bf),
            pltpu.VMEM((8, HD, HD), f32),
            pltpu.VMEM((8, 8, HD), f32),
            pltpu.VMEM((8, 8, HD), f32),
            pltpu.VMEM((8, 8, HD), jnp.int32),
            pltpu.VMEM((8, HD, HD), bf),
            pltpu.VMEM((6, HD, HD), bf),
            pltpu.VMEM((rows, depth), bf),
            pltpu.VMEM(out_weight.shape, bf),
            pltpu.VMEM((rows, width), f32),
            pltpu.VMEM((2, rows, width), bf),
            pltpu.VMEM((2, rows, width), bf),
            pltpu.VMEM((rows, width), bf),
            pltpu.VMEM((rows, width), bf),
            dma((3, 6)), dma((8,)), dma((8,)), dma((2, 8)), dma((2, 8)), dma((2, 8)), dma((2, 8)),
            dma((4, 8)), dma((4, 8)), dma((8,)), dma((6,)), dma, dma((3,)), dma((3,)),
        ],
        compiler_params=pltpu.CompilerParams(
            collective_id=0, has_side_effects=True, vmem_limit_bytes=48 * 1024 * 1024
        ),
    )(image_start, query, keys, values, out_weight)


def solution(mesh):
    placed = (P("seq", "head"), P("seq", "head"), P("seq", "head"), P("head", None), P())
    return jax.shard_map(body, mesh=mesh, in_specs=placed, out_specs=P("seq", "head"), check_vma=False)
```

time: 785 us -> 95.7 us (0.12)
  waiting for transfers between devices: 682 us -> 0 us
  Pallas kernels: 0 us -> 90.1 us
  matrix products: 34.2 us -> 0 us
  local copies, waits for them, and re-layouts: 35.8 us -> 4.14 us
  other arithmetic: 18.2 us -> 0 us
  between operations: 14.1 us -> 0.01 us
    all_gather x1 -> x0, waiting for transfers between devices: 603 us -> none  [body(): block_pair = lax.all_gather(key_value, 'seq', axis=2, tiled=True)]
    pallas_call x0 -> x1, Pallas kernels: none -> 90.1 us  [body(): pl.pallas_call(kernel, out_shape=jax.ShapeDtypeStruct((rows, width), bf),...]
    reduce_scatter x1 -> x0, waiting for transfers between devices: 78.6 us -> none  [body(): lax.psum_scatter(partial_value.astype(jnp.bfloat16), 'head', scatter_dime...]
    another operation x1 -> x0, local copies, waits for them, and re-layouts: 32.6 us -> none
    dot_general x2 -> x0, matrix products: 18.4 us -> none  [the longest x1 13.6 us: compute(): jnp.einsum('hqd,hkd->hqk', query_heads, key_block, preferred_element_type...]
    cond x1 -> x0, matrix products: 15.8 us -> none  [body(): state_now = lax.cond(jnp.any(visible), compute, unchanged, initial)]
    reduce_sum x3 -> x0, other arithmetic: 14 us -> none  [the longest x1 12.5 us: compute(): row_sum = jnp.sum(weights, axis=-1)]
  transfers between devices with their start and end apart: 2 -> 0, of which waited for: 2 -> 0; matrix products, arithmetic and copies ran while one was open for 1% -> 0% of each run, Pallas kernels for 0% -> 0%
where the time goes in v1:
time: 95.7 us; the launch traced here: 94.2 us
  Pallas kernels  90.1 us (94%)
  local copies, waits for them, and re-layouts  4.14 us (4%)
    pallas_call x1, Pallas kernels, body(): pl.pallas_call(kernel, out_shape=jax.ShapeDtypeStruct((rows, width), bf),...  90.1 us
    unnamed x9, local copies, waits for them, and re-layouts  4.14 us

profile of v1, /device:TPU:1, one launch (start us, length us, event | category | flops | bytes accessed | tf_op | source)
XLA Modules:
  0.0 94.2 jit_solution(6756029041667965000)
XLA Ops:
  0.0 0.0 copy-start
  0.0 0.9 copy-done
  0.9 0.0 copy-start.1
  0.9 0.9 copy-done.1
  1.9 0.0 copy-start.2
  1.9 0.9 copy-done.2
  2.8 0.0 copy-start.3
  2.8 0.7 copy-done.3
  3.4 90.1 %shard_map.55 = bf16[128,1024]{1,0:T(8,128)(2,1)S(1)} custom-call(s32[3]{0:T(128)S(1)} %copy-done.3, bf16[128,768]{1,0:T(8,128)(2,1)S(1)} %copy-done, bf16[128,768]{1,0:T(8,128)(2,1)S(1)} %copy-done.1, bf16[128,768]{1,0:T(8,128)(2,1)S(1)} %copy-done.2, bf16[768,4096]{1,0:T(8,128)(2,1)} %w_ref.1), custom_call_target="tpu_custom_call" | custom-call | tf_op jit(solution)/shard_map/pallas_call | solution.py:358
  93.5 0.7 copy.7
Async XLA Ops:
  0.0 0.9 copy-start
  0.9 0.9 copy-start.1
  1.9 0.9 copy-start.2
  2.8 0.7 copy-start.3

commit v2 on v0

v2 whole, which is shorter than its diff:
```python
import jax
import jax.numpy as jnp
from jax import lax
from jax.experimental import pallas as pl
from jax.experimental.pallas import tpu as pltpu
from jax.sharding import PartitionSpec as P

MESH = pl.DeviceIdType.MESH
HD = 128
PATCHES = 1024
NEG = -1e30
SCALE = HD**-0.5
PARTS = 2

BY_QUERY = [(t, z) for t in range(4) for z in range(min(2 * t + 3, 8))]
BY_KEY = [(t, z) for z in range(8) for t in range(4) if z <= 2 * t + 2]
UNITS = [(t, z, 0) for t, z in BY_QUERY] + [(t, z, r) for t, z in BY_KEY for r in (3, 1)] + [(t, z, 2) for t, z in BY_QUERY]
LOOPS = len(UNITS) // 2
WINDOW = 3


def first_use(first, last):
    seen = {}
    for u in range(first, last):
        seen.setdefault(UNITS[u][1], u // 2)
    plan = {}
    for z, i in sorted(seen.items(), reverse=True):
        while i in plan:
            i -= 1
        plan[i] = z
    return {i: z for i, z in plan.items() if i > 0}


TODO = (
    {},
    {3: 4, 6: 5},
    {2: 0, 4: 1, 8: 2, 11: 3, 14: 4, 18: 5},
    first_use(0, 23),
    first_use(23, 69),
    first_use(69, 92),
    {1: 1, 4: 2, 7: 3},
    {37: 0, 40: 1, 43: 2},
)


def place():
    s, h = lax.axis_index("seq"), lax.axis_index("head")
    return s // 8, (s // 2) % 4, s % 2, h // 2, h % 2


def device(z, x, yl, yh, c):
    return ((z * 4 + x) * 2 + yl, yh * 2 + c)


def kernel(
    start_hbm, q_hbm, k_hbm, v_hbm, w_ref, o_ref,
    start_ref, todo, q_ref, k_ref, v_ref, vt, kv, qb, accs, ms, lims, ot, att, wv, own, pair_out, pair_in, cross_out, cross_in,
    s0, s1, p0, p1, al0, al1,
    in_sem, a_send, a_kv, a_q, x_send, x_recv, f_send, f_recv, p_send, p_recv, o_send, o_recv, w_sem,
    pair_send, pair_recv, cross_send, cross_recv,
):
    bf, f32 = jnp.bfloat16, jnp.float32
    z, x, yl, yh, c = place()
    couple = z // 2
    active = (z % 2 == 0) | (yl == couple % 2)
    home_core = z // 4
    head = 3 * (couple % 2) + jnp.where(z % 2 == 1, 2, yl)
    right, left = (x + 1) % 4, (x + 3) % 4
    opposite = (x + 2) % 4
    to_right = device(z, right, yl, yh, c)
    to_left = device(z, left, yl, yh, c)
    to_pair = device(z, x, yl, yh, 1 - c)
    to_cross = device(z, x, yl, 1 - yh, c)

    def remote(src, dst, send, recv, dev):
        return pltpu.make_async_remote_copy(src, dst, send, recv, device_id=dev, device_id_type=MESH)

    def worker(i):
        k, j = 2 * c + i // 3, i % 3
        extra = j == 2
        return 2 * k + jnp.where(extra, 1, 0), jnp.where(extra, k % 2, j)

    def is_own(i):
        wz, wyl = worker(i)
        return (wz == z) & (wyl == yl) & (yl == c)

    def source_is_own(zs):
        return (zs == z) & (yl == c) & (home_core == c)

    def columns(i):
        return pl.ds(pl.multiple_of(i * HD, HD), HD)

    copies = [
        pltpu.make_async_copy(src, dst, in_sem.at[n])
        for n, (src, dst) in enumerate(
            ((v_hbm, v_ref), (k_hbm, k_ref), (q_hbm, q_ref), (start_hbm, start_ref))
        )
    ]
    for copy in copies:
        copy.start()

    barrier = pltpu.get_barrier_semaphore()

    def greet(dev):
        pl.semaphore_signal(barrier, inc=1, device_id=dev, device_id_type=MESH)

    def greet_worker(i, _):
        wz, wyl = worker(i)

        @pl.when(jnp.logical_not(is_own(i)))
        def _():
            greet(device(wz, x, wyl, yh, yl))

        return 0

    @pl.when(active)
    def _():
        def greet_source(n, _):
            zs = (z + 4 + n) % 8

            @pl.when(jnp.logical_not(source_is_own(zs)))
            def _():
                greet(device(zs, x, c, yh, home_core))

            return 0

        lax.fori_loop(0, 8, greet_source, 0)
        greet(to_right)
        greet(to_left)

    lax.fori_loop(0, 6, greet_worker, 0)
    greet(to_pair)
    greet(to_cross)

    w_copy = pltpu.make_async_copy(w_ref, wv, w_sem)
    copies[0].wait()
    for i in range(6):
        vt[i] = v_ref[:, i * HD : (i + 1) * HD].T
    for copy in copies[1:]:
        copy.wait()
    w_copy.start()

    def clear(n, _):
        todo[n] = -1
        return 0

    lax.fori_loop(0, len(TODO) * LOOPS, clear, 0)
    for k, plan in enumerate(TODO):
        for i, value in plan.items():
            todo[k * LOOPS + i] = value
            todo[i] = 0
    lanes = lax.broadcasted_iota(jnp.int32, (1, 2 * HD), 1)
    for t in range(4):
        zq = 2 * t + lanes // HD
        pos = ((zq * 4 + x) * 2 + c) * HD + lanes % HD
        lim = pos
        for n in range(3):
            first = start_ref[n]
            lim = jnp.where((pos >= first) & (pos < first + PATCHES), first + (PATCHES - 1), lim)
        lims[t] = jnp.broadcast_to(lim, (8, 2 * HD))
    ms[...] = jnp.full_like(ms, NEG)
    accs[...] = jnp.zeros_like(accs)

    own_pair = ((yl == c) & (home_core == c) & active).astype(jnp.int32)
    expected = 8 + jnp.where(active, 10, 0) - 2 * own_pair
    pl.semaphore_wait(barrier, expected)

    slot = (z * 4 + x) * 2 + yl

    def pieces(i):
        return (
            (k_ref.at[:, columns(i)], kv.at[0, slot], a_kv.at[z]),
            (vt.at[i], kv.at[1, slot], a_kv.at[z]),
            (q_ref.at[:, columns(i)], qb.at[z], a_q.at[z]),
        )

    def a_copy(i, n):
        wz, wyl = worker(i)
        src, dst, sem = pieces(i)[n]
        return remote(src, dst, a_send.at[n, i], sem, device(wz, x, wyl, yh, yl))

    def a_start(i):
        @pl.when(is_own(i))
        def _():
            for src, dst, sem in pieces(i):
                pltpu.make_async_copy(src, dst, sem).start()

        @pl.when(jnp.logical_not(is_own(i)))
        def _():
            for n in range(3):
                a_copy(i, n).start()

    def a_sent(i):
        @pl.when(jnp.logical_not(is_own(i)))
        def _():
            for n in range(3):
                a_copy(i, n).wait_send()

    def a_round(m):
        @pl.when(m < 6)
        def _():
            @pl.when(m >= WINDOW)
            def _():
                a_sent((m - WINDOW + z) % 6)

            a_start((m + z) % 6)

    @pl.when(jnp.logical_not(active))
    def _():
        def step(m, _):
            a_round(m)
            return 0

        lax.fori_loop(0, 6, step, 0)

    @pl.when(active)
    def _():
        def at(zk, xk, w):
            return (zk * 4 + xk) * 2 + w

        def x_copy(side, b):
            s = at(b, x, c)
            return remote(
                kv.at[:, s], kv.at[:, s], x_send.at[side, b], x_recv.at[side, b], to_right if side == 0 else to_left
            )

        def x_wait(side, b):
            s = at(b, left if side == 0 else right, c)
            remote(
                kv.at[:, s], kv.at[:, s], x_send.at[side, b], x_recv.at[side, b], to_right if side == 0 else to_left
            ).wait_recv()

        def f_copy(side, b):
            s = at(b, left if side == 0 else right, c)
            return remote(
                kv.at[side, s], kv.at[side, s], f_send.at[side, b], f_recv.at[side, b],
                to_right if side == 0 else to_left,
            )

        def f_wait(side, b):
            s = at(b, opposite, c)
            remote(
                kv.at[side, s], kv.at[side, s], f_send.at[side, b], f_recv.at[side, b],
                to_right if side == 0 else to_left,
            ).wait_recv()

        def p_copy(rel, b, w):
            s = at(b, (x + rel) % 4, w)
            return remote(kv.at[:, s], kv.at[:, s], p_send.at[rel, b], p_recv.at[rel, b], to_pair)

        def o_copy(zq):
            return remote(
                ot.at[zq], att.at[:, columns(head)], o_send.at[zq], o_recv.at[head],
                device(zq, x, c, yh, home_core),
            )

        def own_step(b):
            s = at(b, x, c)
            remote(kv.at[:, s], kv.at[:, s], x_send.at[0, b], a_kv.at[b], to_pair).wait_recv()
            x_copy(0, b).start()
            x_copy(1, b).start()
            p_copy(0, b, c).start()

        def side_step(b):
            x_wait(0, b)
            f_copy(0, b).start()
            p_copy(3, b, c).start()
            x_wait(1, b)
            f_copy(1, b).start()
            p_copy(1, b, c).start()

        def far_step(b):
            f_wait(0, b)
            f_wait(1, b)
            p_copy(2, b, c).start()

        def q_wait(t):
            for b in (2 * t, 2 * t + 1):
                remote(qb.at[b], qb.at[b], x_send.at[0, b], a_q.at[b], to_pair).wait_recv()

        scores, weights, scales = (s0, s1), (p0, p1), (al0, al1)
        rows = lax.broadcasted_iota(jnp.int32, (2 * HD, 2 * HD), 0)
        ones = jnp.ones((16, 2 * HD), bf)

        def score(t, b, n):
            k = kv[0, pl.ds(b, 2)].reshape(2 * HD, HD)
            q = qb[pl.ds(2 * t, 2)].reshape(2 * HD, HD)
            scores[n][...] = lax.dot_general(k, q, (((1,), (1,)), ((), ())), preferred_element_type=f32)

        def weigh(t, b, n):
            sc = jnp.where(rows <= lims[t, 0:1] - b * HD, scores[n][...], NEG)
            m = ms[t, 0:1]
            m_new = jnp.maximum(m, jnp.max(sc, axis=0, keepdims=True))
            weights[n][...] = jnp.exp((sc - m_new) * SCALE).astype(bf)
            scales[n][...] = jnp.broadcast_to(jnp.exp((m - m_new) * SCALE), (8, 2 * HD))
            ms[t, 0:1] = m_new

        def gather(t, b, n):
            v = jnp.concatenate([jnp.concatenate([kv[1, b], kv[1, b + 1]], axis=1), ones], axis=0)
            accs[t] = accs[t] * scales[n][0:1] + jnp.dot(v, weights[n][...], preferred_element_type=f32)

        def finish(t):
            total = accs[t]
            done = total[:HD] * (1.0 / total[HD : HD + 1])
            for j in range(2):
                zq = 2 * t + j
                ot[zq] = done[:, j * HD : (j + 1) * HD].T.astype(bf)

                @pl.when(source_is_own(zq))
                def _():
                    pltpu.make_async_copy(ot.at[zq], att.at[:, columns(head)], o_recv.at[head]).start()

                @pl.when(jnp.logical_not(source_is_own(zq)))
                def _():
                    o_copy(zq).start()

        def pair_wait(rels):
            def run(b):
                for rel in rels:
                    p_copy(rel, b, 1 - c).wait_recv()

            return run

        def in_round(step):
            def run(m):
                b = (head + 12 - m) % 6
                step(b)

                @pl.when(b < 2)
                def _():
                    step(b + 6)

            return run

        actions = (in_round(side_step), in_round(far_step), pair_wait((0,)), pair_wait((3, 1)), pair_wait((2,)), q_wait, finish)

        def events(i):
            @pl.when(todo[i] >= 0)
            def _():
                for k, action in enumerate(actions):
                    value = todo[(k + 1) * LOOPS + i]

                    @pl.when(value >= 0)
                    def _():
                        action(value)

        def steps(u, marks):
            n = jnp.int32(0)
            for mark in marks:
                n = n + (u >= mark).astype(jnp.int32)
            return n

        def unit(u):
            u = jnp.asarray(u, jnp.int32)
            by_query = (u < 23) | (u >= 69)
            v = jnp.where(u < 23, u, jnp.where(u < 69, (u - 23) // 2, u - 69))
            tq = steps(v, (3, 8, 15))
            zq = v - tq * (tq + 2)
            zk = steps(v, (4, 8, 12, 15, 18, 20, 22))
            skipped = steps(v, (15, 20, 22))
            low = steps(zk, (3, 5, 7))
            begin = 4 * zk - steps(zk, (4, 5, 6, 6, 7, 7))
            tk = low + v - begin
            rel = jnp.where(u < 23, 0, jnp.where(u >= 69, 2, jnp.where((u - 23) % 2 == 0, 3, 1)))
            t = jnp.where(by_query, tq, tk)
            zz = jnp.where(by_query, zq, zk)
            return t, zz, rel

        def look(u):
            t, zz, rel = unit(u)
            return t, at(zz, (x + rel) % 4, 0)

        for m in range(WINDOW - 1):
            a_round(jnp.int32(m))

        def first(m, _):
            a_round(m + (WINDOW - 1))
            in_round(own_step)(m)

            @pl.when(m >= 2)
            def _():
                in_round(side_step)(m - 2)

            return 0

        lax.fori_loop(0, 6, first, 0)
        q_wait(0)
        pair_wait((0,))(0)
        pair_wait((0,))(1)
        u0, u1 = look(0), look(1)
        score(*u0, 0)
        score(*u1, 1)
        weigh(*u0, 0)

        def two(i, _):
            events(i)
            before, last, now, later = [look(2 * i + n) for n in (-2, -1, 0, 1)]
            score(*now, 0)
            weigh(*last, 1)
            gather(*before, 0)
            score(*later, 1)
            weigh(*now, 0)
            gather(*last, 1)
            return 0

        lax.fori_loop(1, LOOPS, two, 0)
        before, last = look(2 * LOOPS - 2), look(2 * LOOPS - 1)
        weigh(*last, 1)
        gather(*before, 0)
        gather(*last, 1)
        finish(3)

    for i in range(6):
        remote(att.at[:, columns(i)], att.at[:, columns(i)], a_send.at[0, i], o_recv.at[i], to_pair).wait_recv()

    w_copy.wait()
    width = o_ref.shape[1]
    part = width // PARTS

    def project(gy, gc, p):
        first = pl.multiple_of((gy * 2 + gc) * width + p * part, part)
        return jnp.dot(att[...], wv[:, pl.ds(first, part)], preferred_element_type=f32)

    def pair_copy(n, p):
        return remote(pair_out.at[n, p], pair_in.at[n, p], pair_send.at[n, p], pair_recv.at[n, p], to_pair)

    def cross_copy(p):
        return remote(cross_out.at[p], cross_in.at[p], cross_send.at[p], cross_recv.at[p], to_cross)

    for p in range(PARTS):
        pair_out[0, p] = project(1 - yh, 1 - c, p).astype(bf)
        pair_copy(0, p).start()
    for p in range(PARTS):
        own[p] = project(1 - yh, c, p)
        pair_copy(0, p).wait_recv()
        cross_out[p] = (own[p] + pair_in[0, p].astype(f32)).astype(bf)
        cross_copy(p).start()
    for p in range(PARTS):
        pair_out[1, p] = project(yh, 1 - c, p).astype(bf)
        pair_copy(1, p).start()
    for p in range(PARTS):
        own[p] = project(yh, c, p)
        pair_copy(1, p).wait_recv()
        own[p] += pair_in[1, p].astype(f32)
    for p in range(PARTS):
        cross_copy(p).wait_recv()
        o_ref[:, p * part : (p + 1) * part] = (own[p] + cross_in[p].astype(f32)).astype(bf)

    for p in range(PARTS):
        pair_copy(0, p).wait_send()
        pair_copy(1, p).wait_send()
        cross_copy(p).wait_send()

    def a_drain(m, _):
        a_sent((m + z) % 6)
        return 0

    lax.fori_loop(6 - WINDOW, 6, a_drain, 0)

    @pl.when(active)
    def _():
        def drain(b, _):
            for side in (0, 1):
                s = (b * 4 + x) * 2 + c
                to = to_right if side == 0 else to_left
                remote(kv.at[:, s], kv.at[:, s], x_send.at[side, b], x_recv.at[side, b], to).wait_send()
                remote(kv.at[side, s], kv.at[side, s], f_send.at[side, b], f_recv.at[side, b], to).wait_send()
            for rel in range(4):
                s = (b * 4 + (x + rel) % 4) * 2 + c
                remote(kv.at[:, s], kv.at[:, s], p_send.at[rel, b], p_recv.at[rel, b], to_pair).wait_send()

            @pl.when(jnp.logical_not(source_is_own(b)))
            def _():
                remote(
                    ot.at[b], att.at[:, columns(head)], o_send.at[b], o_recv.at[head],
                    device(b, x, c, yh, home_core),
                ).wait_send()

            return 0

        lax.fori_loop(0, 8, drain, 0)


def body(query, keys, values, out_weight, image_start):
    rows, depth = query.shape
    width = out_weight.shape[1] // lax.axis_size("head")
    part = width // PARTS
    bf, f32, dma, hd = jnp.bfloat16, jnp.float32, pltpu.SemaphoreType.DMA, HD
    return pl.pallas_call(
        kernel,
        out_shape=jax.ShapeDtypeStruct((rows, width), bf),
        in_specs=[pl.BlockSpec(memory_space=pl.ANY)] * 5,
        out_specs=pl.BlockSpec(memory_space=pltpu.VMEM),
        scratch_shapes=[
            pltpu.SMEM((3,), jnp.int32),
            pltpu.SMEM((len(TODO) * LOOPS,), jnp.int32),
            pltpu.VMEM((rows, depth), bf),
            pltpu.VMEM((rows, depth), bf),
            pltpu.VMEM((rows, depth), bf),
            pltpu.VMEM((6, hd, hd), bf),
            pltpu.VMEM((2, 64, hd, hd), bf),
            pltpu.VMEM((8, hd, hd), bf),
            pltpu.VMEM((4, hd + 16, 2 * hd), f32),
            pltpu.VMEM((4, 8, 2 * hd), f32),
            pltpu.VMEM((4, 8, 2 * hd), jnp.int32),
            pltpu.VMEM((8, hd, hd), bf),
            pltpu.VMEM((rows, depth), bf),
            pltpu.VMEM(out_weight.shape, bf),
            pltpu.VMEM((PARTS, rows, part), f32),
            pltpu.VMEM((2, PARTS, rows, part), bf),
            pltpu.VMEM((2, PARTS, rows, part), bf),
            pltpu.VMEM((PARTS, rows, part), bf),
            pltpu.VMEM((PARTS, rows, part), bf),
            pltpu.VMEM((2 * hd, 2 * hd), f32),
            pltpu.VMEM((2 * hd, 2 * hd), f32),
            pltpu.VMEM((2 * hd, 2 * hd), bf),
            pltpu.VMEM((2 * hd, 2 * hd), bf),
            pltpu.VMEM((8, 2 * hd), f32),
            pltpu.VMEM((8, 2 * hd), f32),
            dma((4,)), dma((3, 6)), dma((8,)), dma((8,)), dma((2, 8)), dma((2, 8)), dma((2, 8)), dma((2, 8)),
            dma((4, 8)), dma((4, 8)), dma((8,)), dma((6,)), dma,
            dma((2, PARTS)), dma((2, PARTS)), dma((PARTS,)), dma((PARTS,)),
        ],
        compiler_params=pltpu.CompilerParams(
            collective_id=0, has_side_effects=True, vmem_limit_bytes=48 * 1024 * 1024
        ),
    )(image_start, query, keys, values, out_weight)


def solution(mesh):
    placed = (P("seq", "head"), P("seq", "head"), P("seq", "head"), P("head", None), P())
    return jax.shard_map(body, mesh=mesh, in_specs=placed, out_specs=P("seq", "head"), check_vma=False)
```

time: 785 us -> 72.9 us (0.09)
  waiting for transfers between devices: 682 us -> 0 us
  Pallas kernels: 0 us -> 68.1 us
  matrix products: 34.2 us -> 0 us
  local copies, waits for them, and re-layouts: 35.8 us -> 4.14 us
  other arithmetic: 18.2 us -> 0 us
  between operations: 14.1 us -> 0.01 us
    all_gather x1 -> x0, waiting for transfers between devices: 603 us -> none  [body(): block_pair = lax.all_gather(key_value, 'seq', axis=2, tiled=True)]
    reduce_scatter x1 -> x0, waiting for transfers between devices: 78.6 us -> none  [body(): lax.psum_scatter(partial_value.astype(jnp.bfloat16), 'head', scatter_dime...]
    pallas_call x0 -> x1, Pallas kernels: none -> 68.1 us  [body(): pl.pallas_call(kernel, out_shape=jax.ShapeDtypeStruct((rows, width), bf),...]
    another operation x1 -> x0, local copies, waits for them, and re-layouts: 32.6 us -> none
    dot_general x2 -> x0, matrix products: 18.4 us -> none  [the longest x1 13.6 us: compute(): jnp.einsum('hqd,hkd->hqk', query_heads, key_block, preferred_element_type...]
    cond x1 -> x0, matrix products: 15.8 us -> none  [body(): state_now = lax.cond(jnp.any(visible), compute, unchanged, initial)]
    reduce_sum x3 -> x0, other arithmetic: 14 us -> none  [the longest x1 12.5 us: compute(): row_sum = jnp.sum(weights, axis=-1)]
  transfers between devices with their start and end apart: 2 -> 0, of which waited for: 2 -> 0; matrix products, arithmetic and copies ran while one was open for 1% -> 0% of each run, Pallas kernels for 0% -> 0%
where the time goes in v2:
time: 72.9 us; the launch traced here: 72.2 us
  Pallas kernels  68.1 us (93%)
  local copies, waits for them, and re-layouts  4.14 us (6%)
    pallas_call x1, Pallas kernels, body(): pl.pallas_call(kernel, out_shape=jax.ShapeDtypeStruct((rows, width), bf),...  68.1 us
    unnamed x9, local copies, waits for them, and re-layouts  4.14 us

profile of v2, /device:TPU:1, one launch (start us, length us, event | category | flops | bytes accessed | tf_op | source)
XLA Modules:
  0.0 72.2 jit_solution(12873377044647854186)
XLA Ops:
  0.0 0.0 copy-start
  0.0 0.9 %copy-done = bf16[128,768]{1,0:T(8,128)(2,1)S(1)} copy-done((bf16[128,768]{1,0:T(8,128)(2,1)S(1)}, bf16[128,768]{1,0:T(8,128)(2,1)}, u32[]{:S(2)}) %copy-start) | copy-done | bytes 196632
  0.9 0.0 copy-start.1
  0.9 0.9 %copy-done.1 = bf16[128,768]{1,0:T(8,128)(2,1)S(1)} copy-done((bf16[128,768]{1,0:T(8,128)(2,1)S(1)}, bf16[128,768]{1,0:T(8,128)(2,1)}, u32[]{:S(2)}) %copy-start.1) | copy-done | bytes 196632
  1.9 0.0 copy-start.2
  1.9 0.9 %copy-done.2 = bf16[128,768]{1,0:T(8,128)(2,1)S(1)} copy-done((bf16[128,768]{1,0:T(8,128)(2,1)S(1)}, bf16[128,768]{1,0:T(8,128)(2,1)}, u32[]{:S(2)}) %copy-start.2) | copy-done | bytes 196632
  2.8 0.0 copy-start.3
  2.8 0.7 copy-done.3
  3.4 68.1 %shard_map.55 = bf16[128,1024]{1,0:T(8,128)(2,1)S(1)} custom-call(s32[3]{0:T(128)S(1)} %copy-done.3, bf16[128,768]{1,0:T(8,128)(2,1)S(1)} %copy-done, bf16[128,768]{1,0:T(8,128)(2,1)S(1)} %copy-done.1, bf16[128,768]{1,0:T(8,128)(2,1)S(1)} %copy-done.2, bf16[768,4096]{1,0:T(8,128)(2,1)} %w_ref.1), custom_call_target="tpu_custom_call" | custom-call | tf_op jit(solution)/shard_map/pallas_call | solution.py:489
  71.5 0.7 copy.7
Async XLA Ops:
  0.0 0.9 %copy-start = (bf16[128,768]{1,0:T(8,128)(2,1)S(1)}, bf16[128,768]{1,0:T(8,128)(2,1)}, u32[]{:S(2)}) copy-start(bf16[128,768]{1,0:T(8,128)(2,1)} %q_hbm.1) | copy-start | bytes 589828
  0.9 0.9 %copy-start.1 = (bf16[128,768]{1,0:T(8,128)(2,1)S(1)}, bf16[128,768]{1,0:T(8,128)(2,1)}, u32[]{:S(2)}) copy-start(bf16[128,768]{1,0:T(8,128)(2,1)} %k_hbm.1) | copy-start | bytes 589828
  1.9 0.9 %copy-start.2 = (bf16[128,768]{1,0:T(8,128)(2,1)S(1)}, bf16[128,768]{1,0:T(8,128)(2,1)}, u32[]{:S(2)}) copy-start(bf16[128,768]{1,0:T(8,128)(2,1)} %v_hbm.1) | copy-start | bytes 589828
  2.8 0.7 copy-start.3

commit v3 on v2

--- a/solution.py
+++ b/solution.py
@@ -16,7 +16,7 @@
 BY_KEY = [(t, z) for z in range(8) for t in range(4) if z <= 2 * t + 2]
 UNITS = [(t, z, 0) for t, z in BY_QUERY] + [(t, z, r) for t, z in BY_KEY for r in (3, 1)] + [(t, z, 2) for t, z in BY_QUERY]
 LOOPS = len(UNITS) // 2
-WINDOW = 3
+WINDOW = 4
 
 
 def first_use(first, last):
@@ -33,8 +33,8 @@
 
 TODO = (
     {},
-    {3: 4, 6: 5},
-    {2: 0, 4: 1, 8: 2, 11: 3, 14: 4, 18: 5},
+    {1: 0, 2: 1, 3: 2, 4: 3, 5: 4, 6: 5},
+    {7: 0, 9: 1, 11: 2, 13: 3, 15: 4, 18: 5},
     first_use(0, 23),
     first_use(23, 69),
     first_use(69, 92),
@@ -140,27 +140,6 @@
         copy.wait()
     w_copy.start()
 
-    def clear(n, _):
-        todo[n] = -1
-        return 0
-
-    lax.fori_loop(0, len(TODO) * LOOPS, clear, 0)
-    for k, plan in enumerate(TODO):
-        for i, value in plan.items():
-            todo[k * LOOPS + i] = value
-            todo[i] = 0
-    lanes = lax.broadcasted_iota(jnp.int32, (1, 2 * HD), 1)
-    for t in range(4):
-        zq = 2 * t + lanes // HD
-        pos = ((zq * 4 + x) * 2 + c) * HD + lanes % HD
-        lim = pos
-        for n in range(3):
-            first = start_ref[n]
-            lim = jnp.where((pos >= first) & (pos < first + PATCHES), first + (PATCHES - 1), lim)
-        lims[t] = jnp.broadcast_to(lim, (8, 2 * HD))
-    ms[...] = jnp.full_like(ms, NEG)
-    accs[...] = jnp.zeros_like(accs)
-
     own_pair = ((yl == c) & (home_core == c) & active).astype(jnp.int32)
     expected = 8 + jnp.where(active, 10, 0) - 2 * own_pair
     pl.semaphore_wait(barrier, expected)
@@ -179,21 +158,22 @@
         src, dst, sem = pieces(i)[n]
         return remote(src, dst, a_send.at[n, i], sem, device(wz, x, wyl, yh, yl))
 
-    def a_start(i):
+    def a_start(i, ns):
         @pl.when(is_own(i))
         def _():
-            for src, dst, sem in pieces(i):
+            for n in ns:
+                src, dst, sem = pieces(i)[n]
                 pltpu.make_async_copy(src, dst, sem).start()
 
         @pl.when(jnp.logical_not(is_own(i)))
         def _():
-            for n in range(3):
+            for n in ns:
                 a_copy(i, n).start()
 
-    def a_sent(i):
+    def a_sent(i, ns):
         @pl.when(jnp.logical_not(is_own(i)))
         def _():
-            for n in range(3):
+            for n in ns:
                 a_copy(i, n).wait_send()
 
     def a_round(m):
@@ -201,9 +181,17 @@
         def _():
             @pl.when(m >= WINDOW)
             def _():
-                a_sent((m - WINDOW + z) % 6)
-
-            a_start((m + z) % 6)
+                a_sent((m - WINDOW + z) % 6, (0, 1))
+
+            a_start((m + z) % 6, (0, 1))
+
+        @pl.when(m == 6)
+        def _():
+            def all_q(n, _):
+                a_start((n + z) % 6, (2,))
+                return 0
+
+            lax.fori_loop(0, 6, all_q, 0)
 
     @pl.when(jnp.logical_not(active))
     def _():
@@ -211,7 +199,7 @@
             a_round(m)
             return 0
 
-        lax.fori_loop(0, 6, step, 0)
+        lax.fori_loop(0, 7, step, 0)
 
     @pl.when(active)
     def _():
@@ -373,13 +361,31 @@
         for m in range(WINDOW - 1):
             a_round(jnp.int32(m))
 
+        def clear(n, _):
+            for k in range(len(TODO)):
+                todo[k * LOOPS + n] = -1
+            return 0
+
+        lax.fori_loop(0, LOOPS, clear, 0)
+        for k, plan in enumerate(TODO):
+            for i, value in plan.items():
+                todo[k * LOOPS + i] = value
+                todo[i] = 0
+        lanes = lax.broadcasted_iota(jnp.int32, (1, 2 * HD), 1)
+        for t in range(4):
+            zq = 2 * t + lanes // HD
+            pos = ((zq * 4 + x) * 2 + c) * HD + lanes % HD
+            lim = pos
+            for n in range(3):
+                first = start_ref[n]
+                lim = jnp.where((pos >= first) & (pos < first + PATCHES), first + (PATCHES - 1), lim)
+            lims[t] = jnp.broadcast_to(lim, (8, 2 * HD))
+        ms[...] = jnp.full_like(ms, NEG)
+        accs[...] = jnp.zeros_like(accs)
+
         def first(m, _):
             a_round(m + (WINDOW - 1))
             in_round(own_step)(m)
-
-            @pl.when(m >= 2)
-            def _():
-                in_round(side_step)(m - 2)
 
             return 0
 
@@ -452,10 +458,15 @@
         cross_copy(p).wait_send()
 
     def a_drain(m, _):
-        a_sent((m + z) % 6)
+        a_sent((m + z) % 6, (2,))
+
+        @pl.when(m >= 6 - WINDOW)
+        def _():
+            a_sent((m + z) % 6, (0, 1))
+
         return 0
 
-    lax.fori_loop(6 - WINDOW, 6, a_drain, 0)
+    lax.fori_loop(0, 6, a_drain, 0)
 
     @pl.when(active)
     def _():

time: 72.9 us -> 68.9 us (0.945)
  Pallas kernels: 68.1 us -> 64.6 us
    pallas_call x1, Pallas kernels: 68.1 us -> 64.6 us  [body(): pl.pallas_call(kernel, out_shape=jax.ShapeDtypeStruct((rows, width), bf),...]
where the time goes in v3:
time: 68.9 us; the launch traced here: 68.7 us
  Pallas kernels  64.6 us (94%)
  local copies, waits for them, and re-layouts  4.14 us (6%)
    pallas_call x1, Pallas kernels, body(): pl.pallas_call(kernel, out_shape=jax.ShapeDtypeStruct((rows, width), bf),...  64.6 us
    unnamed x9, local copies, waits for them, and re-layouts  4.14 us

profile of v3, /device:TPU:1, one launch (start us, length us, event | category | flops | bytes accessed | tf_op | source)
XLA Modules:
  0.0 68.7 jit_solution(11894270934875874902)
XLA Ops:
  0.0 0.0 copy-start
  0.0 0.9 %copy-done = bf16[128,768]{1,0:T(8,128)(2,1)S(1)} copy-done((bf16[128,768]{1,0:T(8,128)(2,1)S(1)}, bf16[128,768]{1,0:T(8,128)(2,1)}, u32[]{:S(2)}) %copy-start) | copy-done | bytes 196632
  0.9 0.0 copy-start.1
  0.9 0.9 %copy-done.1 = bf16[128,768]{1,0:T(8,128)(2,1)S(1)} copy-done((bf16[128,768]{1,0:T(8,128)(2,1)S(1)}, bf16[128,768]{1,0:T(8,128)(2,1)}, u32[]{:S(2)}) %copy-start.1) | copy-done | bytes 196632
  1.9 0.0 copy-start.2
  1.9 0.9 %copy-done.2 = bf16[128,768]{1,0:T(8,128)(2,1)S(1)} copy-done((bf16[128,768]{1,0:T(8,128)(2,1)S(1)}, bf16[128,768]{1,0:T(8,128)(2,1)}, u32[]{:S(2)}) %copy-start.2) | copy-done | bytes 196632
  2.8 0.0 copy-start.3
  2.8 0.7 copy-done.3
  3.4 64.6 %shard_map.55 = bf16[128,1024]{1,0:T(8,128)(2,1)S(1)} custom-call(s32[3]{0:T(128)S(1)} %copy-done.3, bf16[128,768]{1,0:T(8,128)(2,1)S(1)} %copy-done, bf16[128,768]{1,0:T(8,128)(2,1)S(1)} %copy-done.1, bf16[128,768]{1,0:T(8,128)(2,1)S(1)} %copy-done.2, bf16[768,4096]{1,0:T(8,128)(2,1)} %w_ref.1), custom_call_target="tpu_custom_call" | custom-call | tf_op jit(solution)/shard_map/pallas_call | solution.py:500
  68.0 0.7 %copy.7 = bf16[128,1024]{1,0:T(8,128)(2,1)} copy(bf16[128,1024]{1,0:T(8,128)(2,1)S(1)} %shard_map.55) | data formatting | bytes 524288
Async XLA Ops:
  0.0 0.9 %copy-start = (bf16[128,768]{1,0:T(8,128)(2,1)S(1)}, bf16[128,768]{1,0:T(8,128)(2,1)}, u32[]{:S(2)}) copy-start(bf16[128,768]{1,0:T(8,128)(2,1)} %q_hbm.1) | copy-start | bytes 589828
  0.9 0.9 %copy-start.1 = (bf16[128,768]{1,0:T(8,128)(2,1)S(1)}, bf16[128,768]{1,0:T(8,128)(2,1)}, u32[]{:S(2)}) copy-start(bf16[128,768]{1,0:T(8,128)(2,1)} %k_hbm.1) | copy-start | bytes 589828
  1.9 0.9 %copy-start.2 = (bf16[128,768]{1,0:T(8,128)(2,1)S(1)}, bf16[128,768]{1,0:T(8,128)(2,1)}, u32[]{:S(2)}) copy-start(bf16[128,768]{1,0:T(8,128)(2,1)} %v_hbm.1) | copy-start | bytes 589828
  2.8 0.7 copy-start.3

commit v4 on v3

--- a/solution.py
+++ b/solution.py
@@ -185,7 +185,7 @@
 
             a_start((m + z) % 6, (0, 1))
 
-        @pl.when(m == 6)
+        @pl.when(m == 8)
         def _():
             def all_q(n, _):
                 a_start((n + z) % 6, (2,))
@@ -199,7 +199,7 @@
             a_round(m)
             return 0
 
-        lax.fori_loop(0, 7, step, 0)
+        lax.fori_loop(0, 9, step, 0)
 
     @pl.when(active)
     def _():

time: 68.9 us -> 68.7 us (level)
  no operation moved by 1% of the time
where the time goes in v4:
time: 68.7 us; the launch traced here: 68.4 us
  Pallas kernels  64.3 us (94%)
  local copies, waits for them, and re-layouts  4.14 us (6%)
    pallas_call x1, Pallas kernels, body(): pl.pallas_call(kernel, out_shape=jax.ShapeDtypeStruct((rows, width), bf),...  64.3 us
    unnamed x9, local copies, waits for them, and re-layouts  4.14 us

profile of v4, /device:TPU:1, one launch (start us, length us, event | category | flops | bytes accessed | tf_op | source)
XLA Modules:
  0.0 68.4 jit_solution(5167321837835125016)
XLA Ops:
  0.0 0.0 copy-start
  0.0 0.9 %copy-done = bf16[128,768]{1,0:T(8,128)(2,1)S(1)} copy-done((bf16[128,768]{1,0:T(8,128)(2,1)S(1)}, bf16[128,768]{1,0:T(8,128)(2,1)}, u32[]{:S(2)}) %copy-start) | copy-done | bytes 196632
  0.9 0.0 copy-start.1
  0.9 0.9 %copy-done.1 = bf16[128,768]{1,0:T(8,128)(2,1)S(1)} copy-done((bf16[128,768]{1,0:T(8,128)(2,1)S(1)}, bf16[128,768]{1,0:T(8,128)(2,1)}, u32[]{:S(2)}) %copy-start.1) | copy-done | bytes 196632
  1.9 0.0 copy-start.2
  1.9 0.9 %copy-done.2 = bf16[128,768]{1,0:T(8,128)(2,1)S(1)} copy-done((bf16[128,768]{1,0:T(8,128)(2,1)S(1)}, bf16[128,768]{1,0:T(8,128)(2,1)}, u32[]{:S(2)}) %copy-start.2) | copy-done | bytes 196632
  2.8 0.0 copy-start.3
  2.8 0.7 copy-done.3
  3.4 64.3 %shard_map.55 = bf16[128,1024]{1,0:T(8,128)(2,1)S(1)} custom-call(s32[3]{0:T(128)S(1)} %copy-done.3, bf16[128,768]{1,0:T(8,128)(2,1)S(1)} %copy-done, bf16[128,768]{1,0:T(8,128)(2,1)S(1)} %copy-done.1, bf16[128,768]{1,0:T(8,128)(2,1)S(1)} %copy-done.2, bf16[768,4096]{1,0:T(8,128)(2,1)} %w_ref.1), custom_call_target="tpu_custom_call" | custom-call | tf_op jit(solution)/shard_map/pallas_call | solution.py:500
  67.7 0.7 %copy.7 = bf16[128,1024]{1,0:T(8,128)(2,1)} copy(bf16[128,1024]{1,0:T(8,128)(2,1)S(1)} %shard_map.55) | data formatting | bytes 524288
Async XLA Ops:
  0.0 0.9 %copy-start = (bf16[128,768]{1,0:T(8,128)(2,1)S(1)}, bf16[128,768]{1,0:T(8,128)(2,1)}, u32[]{:S(2)}) copy-start(bf16[128,768]{1,0:T(8,128)(2,1)} %q_hbm.1) | copy-start | bytes 589828
  0.9 0.9 %copy-start.1 = (bf16[128,768]{1,0:T(8,128)(2,1)S(1)}, bf16[128,768]{1,0:T(8,128)(2,1)}, u32[]{:S(2)}) copy-start(bf16[128,768]{1,0:T(8,128)(2,1)} %k_hbm.1) | copy-start | bytes 589828
  1.9 0.9 %copy-start.2 = (bf16[128,768]{1,0:T(8,128)(2,1)S(1)}, bf16[128,768]{1,0:T(8,128)(2,1)}, u32[]{:S(2)}) copy-start(bf16[128,768]{1,0:T(8,128)(2,1)} %v_hbm.1) | copy-start | bytes 589828
  2.8 0.7 copy-start.3
